TPU v7x, 32 devices: a whole 2x2x4 slice. The times are simulated.
32 devices in a mesh: row: 16 (over z, y, x), col: 2 (over core).
Axes of the slice: x: 2, y: 2, z: 4, core: 2. Of those that a mesh axis runs over, the one named last changes fastest.
Arguments:
- matrix: float32 [2, 16, 4, 2, 256, 256], P(None, 'row', None, 'col'), as said below
- keep_mask: int32 [2, 16, 4, 2], P(None, 'row', None, 'col'), may hold values 0 or 1
Outputs:
- factored: float32 [2, 16, 4, 2, 256, 256], P(None, 'row', None, 'col')
Inputs may be any that keep to these rules, and one draw needn't show every extreme that they name: `matrix`: tiles whose row and column index are equal are symmetric, and the symmetric completion of the kept tiles in the window's leading two tile rows and columns is positive definite, so that both panel steps meet positive definite diagonal tiles.
All inputs are finite; a program needn't handle non-finite values. No bound on the sum of `keep_mask` on one device may be relied on, other than what follows from the above.
Results may differ from a plain program's by a relative error of at most 0.0001.
Values sent between devices are 32-bit elements; how exact they have to be, the bound alone decides.
No kernel may reach another device: no remote copies, remote signals or barrier semaphores. Data moves between devices by JAX's collectives and lax.ppermute only.
A program may use at most 64 MiB of HBM per device.

v0:
```python
import jax
import jax.numpy as jnp
from jax import lax
from jax.sharding import PartitionSpec as P

HALF_BAND = 256


def broadcast(shard, axis, root):
    mine = lax.axis_index(axis) == root
    return lax.psum(jnp.where(mine, shard, jnp.zeros_like(shard)), axis)


def right_solve(factor_diag, blocks):
    block_count, tile_edge = (blocks.shape[0], blocks.shape[1])
    stacked = jnp.transpose(blocks, (2, 0, 1)).reshape(tile_edge, block_count * tile_edge)
    solved = lax.linalg.triangular_solve(factor_diag, stacked, left_side=True, lower=True)
    return jnp.transpose(solved.reshape(tile_edge, block_count, tile_edge), (1, 2, 0))


def local(matrix, keep_mask):
    blocks = matrix[:, 0, :, 0]
    kept_marks = keep_mask[:, 0, :, 0]
    row_count, pair_count, tile_edge = (blocks.shape[0], blocks.shape[1], blocks.shape[-1])
    row_devices = lax.axis_size("row")
    row_place = lax.axis_index("row")
    col_place = lax.axis_index("col")
    tile_row = jnp.arange(row_count, dtype=jnp.int32)[:, None] * row_devices + row_place
    tile_col = 2 * jnp.arange(pair_count, dtype=jnp.int32)[None, :] + col_place
    kept_tile = (
        ((kept_marks == 1) | (tile_row == tile_col))
        & (tile_row >= tile_col)
        & (tile_row - tile_col <= HALF_BAND)
    )
    blocks = jnp.where(kept_tile[:, :, None, None], blocks, 0.0)
    lower_part = tile_row >= tile_col
    identity = jnp.eye(tile_edge, dtype=jnp.float32)
    row_index = tile_row[:, 0][:, None, None]
    for panel_step in range(2):
        diag_block = broadcast(blocks[0, 0], "row", panel_step)
        factor_diag = jnp.linalg.cholesky(jnp.where(col_place == panel_step, diag_block, identity))
        solved = right_solve(factor_diag, blocks[:, 0])
        factor_panel_col = jnp.where(
            row_index > panel_step,
            solved,
            jnp.where(row_index == panel_step, factor_diag[None], 0.0),
        )
        factor_panel_col = broadcast(factor_panel_col, "col", panel_step)
        unused = jnp.zeros((tile_edge, tile_edge), jnp.float32)
        leading = [unused for source in range(panel_step + 1)]
        trailing = [
            broadcast(factor_panel_col[0], "row", source)
            for source in range(panel_step + 1, 2 * pair_count)
        ]
        factor_column_set = jnp.stack(leading + trailing)
        column = jnp.where(col_place == panel_step, factor_panel_col, blocks[:, 0])
        blocks = blocks.at[:, 0].set(column)
        paired = factor_column_set.reshape(pair_count, 2, tile_edge, tile_edge)
        my_columns = jnp.where(col_place == 0, paired[:, 0], paired[:, 1])
        product = jnp.einsum(
            "tab,scb->tsac",
            factor_panel_col,
            my_columns,
            precision=lax.Precision.HIGHEST,
            preferred_element_type=jnp.float32,
        )
        selected = (lower_part & (tile_col > panel_step))[:, 0:pair_count, None, None]
        updated = blocks - jnp.where(selected, product, 0.0)
        blocks = jnp.concatenate([blocks[:, :0], updated, blocks[:, pair_count:]], axis=1)
    return blocks[:, None, :, None]


def solution(mesh):
    return jax.shard_map(
        local,
        mesh=mesh,
        in_specs=(P(None, "row", None, "col", None, None), P(None, "row", None, "col")),
        out_specs=P(None, "row", None, "col", None, None),
        check_vma=False,
    )
```

profile of v0, /device:TPU:0, one launch (start us, length us, event | category | flops | bytes accessed | tf_op | source)
XLA Modules:
  0.0 718.5 jit_solution(1143109675651483619)
XLA Ops:
  6.6 2.9 copy.20
  9.5 1.9 bitcast_select_fusion.2
  13.8 108.2 %all-reduce.10.cloned.1.call-done = f32[256,256]{0,1:T(8,128)} async-done(((f32[256,256]{0,1:T(8,128)}), f32[256,256]{0,1:T(8,128)}) %all-reduce.10.cloned.1.call-update) | async-done | bytes 262160 | tf_op jit(solution)/shard_map/psum | solution.py:11
  125.6 11.7 %cholesky.130 = f32[128,128]{1,0:T(8,128)S(1)} custom-call(f32[128,128]{1,0:T(8,128)S(1)} %cholesky.194), custom_call_target="Cholesky" | custom-call | tf_op jit(solution)/shard_map/jit(cholesky)/cholesky | solution.py:41
  137.9 9.8 %custom-call.13 = f32[1,128,128]{1,2,0:T(8,128)S(1)} custom-call(f32[1,128,128]{2,1,0:T(8,128)S(1)} %get-tuple-element.112), custom_call_target="InvertDiagBlocksLowerTriangular" | custom-call | tf_op jit(solution)/shard_map/jit(cholesky)/cholesky | solution.py:41
  149.9 11.7 %cholesky.147 = f32[128,128]{1,0:T(8,128)S(1)} custom-call(f32[128,128]{1,0:T(8,128)S(1)} %convolution_subtract_fusion.3), custom_call_target="Cholesky" | custom-call | tf_op jit(solution)/shard_map/jit(cholesky)/cholesky | solution.py:41
  161.6 1.4 compare_reduce_fusion.3
  165.1 1.7 fusion.27
  166.8 1.2 broadcast.416
  168.1 5.5 while.6
  169.8 1.3 bitcast_dynamic-update-slice_fusion.4
  172.3 1.3 bitcast_dynamic-update-slice_fusion.4
  174.2 20.5 %custom-call.14 = f32[2,128,128]{1,2,0:T(8,128)S(1)} custom-call(f32[2,128,128]{2,1,0:T(8,128)} %copy-done.13), custom_call_target="InvertDiagBlocksLowerTriangular" | custom-call | tf_op jit(solution)/shard_map/triangular_solve/custom-call.0 | solution.py:17
  197.3 1.2 copy.25
  199.3 1.9 fusion.14
  201.3 17.8 %all-reduce.12.cloned.1.call-done = f32[2,256,256]{1,2,0:T(8,128)} async-done(((f32[2,256,256]{1,2,0:T(8,128)}), f32[2,256,256]{1,2,0:T(8,128)}) %all-reduce.12.cloned.1.call-update) | async-done | bytes 524304 | tf_op jit(solution)/shard_map/psum | solution.py:11
  219.1 2.3 slice_select_fusion.8
  222.3 129.0 %all-reduce.20.cloned.1.call-done = (f32[1,256,256]{1,2,0:T(8,128)}, f32[1,256,256]{1,2,0:T(8,128)}, f32[1,256,256]{1,2,0:T(8,128)}, f32[1,256,256]{1,2,0:T(8,12...) async-done(((f32[1,256,256]{1,2,0:T(8,128)}, f32[1,256,256]{1,2,0:T(8,128)}, f32[1,256,256]{1,2,0:T(8,128)}, f32[1,256,256]{1,2,0:T(8,128)}, ...) | async-done | bytes 1835024 | tf_op jit(solution)/shard_map/psum | solution.py:11
  351.3 1.7 constant_dynamic-update-slice_fusion.6
  353.0 1.7 constant_dynamic-update-slice_fusion.5
  354.7 1.7 constant_dynamic-update-slice_fusion.4
  356.4 1.7 constant_dynamic-update-slice_fusion.3
  360.2 3.0 fusion.44
  363.2 1.6 copy.53
  364.8 2.5 copy.54
  367.3 3.0 fusion.2
  370.3 1.3 copy-done
  372.6 1.1 fusion.43
  374.0 104.6 %all-reduce.14.cloned.1.call-done = f32[256,256]{0,1:T(8,128)} async-done(((f32[256,256]{0,1:T(8,128)}), f32[256,256]{0,1:T(8,128)}) %all-reduce.14.cloned.1.call-update) | async-done | bytes 262160 | tf_op jit(solution)/shard_map/psum | solution.py:11
  478.8 11.7 %cholesky.164 = f32[128,128]{1,0:T(8,128)S(1)} custom-call(f32[128,128]{1,0:T(8,128)S(1)} %cholesky.197), custom_call_target="Cholesky" | custom-call | tf_op jit(solution)/shard_map/jit(cholesky)/cholesky | solution.py:41
  490.5 9.8 %custom-call.15 = f32[1,128,128]{1,2,0:T(8,128)S(1)} custom-call(f32[1,128,128]{2,1,0:T(8,128)S(1)} %get-tuple-element.108), custom_call_target="InvertDiagBlocksLowerTriangular" | custom-call | tf_op jit(solution)/shard_map/jit(cholesky)/cholesky | solution.py:41
  500.8 11.7 %cholesky.181 = f32[128,128]{1,0:T(8,128)S(1)} custom-call(f32[128,128]{1,0:T(8,128)S(1)} %convolution_subtract_fusion.2), custom_call_target="Cholesky" | custom-call | tf_op jit(solution)/shard_map/jit(cholesky)/cholesky | solution.py:41
  515.5 4.5 while.7
  516.4 1.5 bitcast_dynamic-update-slice_fusion.5
  518.5 1.5 bitcast_dynamic-update-slice_fusion.5
  520.0 19.7 %custom-call.16 = f32[2,128,128]{1,2,0:T(8,128)S(1)} custom-call(f32[2,128,128]{2,1,0:T(8,128)S(1)} %get-tuple-element.46), custom_call_target="InvertDiagBlocksLowerTriangular" | custom-call | tf_op jit(solution)/shard_map/triangular_solve/custom-call.0 | solution.py:17
  542.8 17.8 %all-reduce.16.cloned.1.call-done = f32[2,256,256]{1,2,0:T(8,128)} async-done(((f32[2,256,256]{1,2,0:T(8,128)}), f32[2,256,256]{1,2,0:T(8,128)}) %all-reduce.16.cloned.1.call-update) | async-done | bytes 524304 | tf_op jit(solution)/shard_map/psum | solution.py:11
  560.6 2.2 slice_select_fusion.2
  563.8 125.2 %all-reduce.18.cloned.1.call-done = (f32[1,256,256]{1,2,0:T(8,128)}, f32[1,256,256]{1,2,0:T(8,128)}, f32[1,256,256]{1,2,0:T(8,128)}, f32[1,256,256]{1,2,0:T(8,12...) async-done(((f32[1,256,256]{1,2,0:T(8,128)}, f32[1,256,256]{1,2,0:T(8,128)}, f32[1,256,256]{1,2,0:T(8,128)}, f32[1,256,256]{1,2,0:T(8,128)}, f32[1,256,256]{1,2,0:T(8,128)}, ...) | async-done | bytes 1572880 | tf_op jit(solution)/shard_map/psum | solution.py:11
  689.0 1.7 constant_dynamic-update-slice_fusion.12
  690.7 1.7 constant_dynamic-update-slice_fusion.11
  692.4 1.7 constant_dynamic-update-slice_fusion.10
  694.0 1.7 constant_dynamic-update-slice_fusion.9
  697.2 3.0 fusion.42
  700.2 1.6 copy.56
  701.7 2.5 copy.57
  704.3 4.3 fusion.1
  708.5 2.9 copy.42
  (111 shorter events, 29.3 us)
Async XLA Ops:
  6.5 115.5 %all-reduce.10.cloned.1.call-start = ((), (), s32[]{:S(2)}) async-start(), calls=%async_computation | async-start | bytes 524288 | tf_op jit(solution)/shard_map/psum | solution.py:11
  6.5 2.9 copy-start.14
  12.2 207.0 %all-reduce.12.cloned.1.call-start = ((), (), s32[]{:S(2)}) async-start(), calls=%async_computation.1 | async-start | bytes 1048576 | tf_op jit(solution)/shard_map/psum | solution.py:11
  123.0 71.7 %copy-start.4 = (f32[256,2,256]{0,2,1:T(8,128)S(1)}, f32[256,2,256]{0,2,1:T(8,128)}, u32[]{:S(2)}) copy-start(f32[256,2,256]{0,2,1:T(8,128)} %copy.23) | copy-start | bytes 1572868
  124.9 0.7 copy-start.7
  163.0 2.1 copy-start.5
  173.6 0.6 copy-start.13
  195.8 2.7 copy-start.6
  201.2 150.1 %all-reduce.20.cloned.1.call-start = ((), (), s32[]{:S(2)}) async-start(), calls=%async_computation.5 | async-start | bytes 3670016 | tf_op jit(solution)/shard_map/psum | solution.py:11
  219.1 3.1 copy-start.2
  221.4 257.1 %all-reduce.14.cloned.1.call-start = ((), (), s32[]{:S(2)}) async-start(), calls=%async_computation.2 | async-start | bytes 524288 | tf_op jit(solution)/shard_map/psum | solution.py:11
  351.3 6.8 copy-start.10
  351.3 7.5 %copy-start.9 = (f32[1,256,256]{1,2,0:T(8,128)S(1)}, f32[1,256,256]{1,2,0:T(8,128)}, u32[]{:S(2)}) copy-start(f32[1,256,256]{1,2,0:T(8,128)} %get-tuple-element.74) | copy-start | bytes 786436
  351.3 8.2 %copy-start.8 = (f32[1,256,256]{1,2,0:T(8,128)S(1)}, f32[1,256,256]{1,2,0:T(8,128)}, u32[]{:S(2)}) copy-start(f32[1,256,256]{1,2,0:T(8,128)} %get-tuple-element.75) | copy-start | bytes 786436
  370.3 1.3 copy-start
  372.4 188.2 %all-reduce.16.cloned.1.call-start = ((), (), s32[]{:S(2)}) async-start(), calls=%async_computation.3 | async-start | bytes 1048576 | tf_op jit(solution)/shard_map/psum | solution.py:11
  373.9 141.5 %copy-start.15 = (s32[2,2]{1,0:T(2,128)S(1)}, s32[2,2]{1,0:T(2,128)}, u32[]{:S(2)}) copy-start(s32[2,2]{1,0:T(2,128)} %get-tuple-element.288) | copy-start | bytes 52
  542.7 21.0 %copy-start.1 = (f32[2,4,256,256]{2,3,1,0:T(8,128)S(1)}, f32[2,4,256,256]{2,3,1,0:T(8,128)}, u32[]{:S(2)}) copy-start(f32[2,4,256,256]{2,3,1,0:T(8,128)} %copy-done) | copy-start | bytes 6291460
  542.7 146.3 %all-reduce.18.cloned.1.call-start = ((), (), s32[]{:S(2)}) async-start(), calls=%async_computation.4 | async-start | bytes 3145728 | tf_op jit(solution)/shard_map/psum | solution.py:11
  560.6 3.1 copy-start.3
  689.0 6.7 copy-start.12
  689.0 7.5 %copy-start.11 = (f32[1,256,256]{1,2,0:T(8,128)S(1)}, f32[1,256,256]{1,2,0:T(8,128)}, u32[]{:S(2)}) copy-start(f32[1,256,256]{1,2,0:T(8,128)} %get-tuple-element.68) | copy-start | bytes 786436
Sparse Core Ops, SparseCore 0:
  12.6 109.3 all-reduce.9
  201.4 17.7 all-reduce.11
  225.6 125.6 all-reduce.19
  372.5 105.9 all-reduce.13
  542.8 17.7 all-reduce.15
  567.9 121.0 all-reduce.17
where the time goes:
time: 728 us; the launch traced here: 718 us
  waiting for transfers between devices  503 us (69%)
  other arithmetic  126 us (17%)
  local copies, waits for them, and re-layouts  58.8 us (8%)
  between operations  16.9 us (2%)
  matrix products  12.7 us (2%)
    psum x6, waiting for transfers between devices, broadcast(): return lax.psum(jnp.where(mine, shard, jnp.zeros_like(shard)), axis)  503 us
    another operation x14, other arithmetic, local(): jnp.linalg.cholesky(jnp.where(col_place == panel_step, diag_block, identi...  70.6 us
    another operation x7, other arithmetic, right_solve(): lax.linalg.triangular_solve(factor_diag, stacked, left_side=True, lower=T...  42.5 us
    unnamed x50, local copies, waits for them, and re-layouts  31 us
  transfers between devices with their start and end apart: 6, of which 6 were waited for; matrix products, arithmetic and copies ran while one was open for 1% of the time, Pallas kernels for 0%

commit v1 on v0

--- a/solution.py
+++ b/solution.py
@@ -8,7 +8,12 @@
 
 def broadcast(shard, axis, root):
     mine = lax.axis_index(axis) == root
-    return lax.psum(jnp.where(mine, shard, jnp.zeros_like(shard)), axis)
+
+    def order_pipes(block_here):
+        low = lax.all_gather(block_here, axis).sum(axis=0)
+        return low
+
+    return order_pipes(jnp.where(mine, shard, jnp.zeros_like(shard)))
 
 
 def right_solve(factor_diag, blocks):

time: 728 us -> 1370 us (1.88)
  waiting for transfers between devices: 503 us -> 1130 us
  other arithmetic: 126 us -> 164 us
  local copies, waits for them, and re-layouts: 58.8 us -> 24.4 us
    all_gather x0 -> x17, waiting for transfers between devices: none -> 1130 us  [order_pipes(): low = lax.all_gather(block_here, axis).sum(axis=0)]
    psum x6 -> x0, waiting for transfers between devices: 503 us -> none  [broadcast(): return lax.psum(jnp.where(mine, shard, jnp.zeros_like(shard)), axis)]
    reduce_sum x0 -> x17, other arithmetic: none -> 41.2 us  [order_pipes(): low = lax.all_gather(block_here, axis).sum(axis=0)]
    unnamed x50 -> x23, local copies, waits for them, and re-layouts: 31 us -> 10.7 us
  transfers between devices with their start and end apart: 6 -> 17, of which waited for: 6 -> 17; matrix products, arithmetic and copies ran while one was open for 1% -> 3% of each run, Pallas kernels for 0% -> 0%
where the time goes in v1:
time: 1370 us; the launch traced here: 1360 us
  waiting for transfers between devices  1130 us (82%)
  other arithmetic  164 us (12%)
  local copies, waits for them, and re-layouts  24.4 us (2%)
  between operations  16.7 us (1%)
  matrix products  14.4 us (1%)
    all_gather x17, waiting for transfers between devices, order_pipes(): low = lax.all_gather(block_here, axis).sum(axis=0)  1130 us
    another operation x14, other arithmetic, local(): jnp.linalg.cholesky(jnp.where(col_place == panel_step, diag_block, identi...  69.3 us
    reduce_sum x17, other arithmetic, order_pipes(): low = lax.all_gather(block_here, axis).sum(axis=0)  41.2 us
    another operation x7, other arithmetic, right_solve(): lax.linalg.triangular_solve(factor_diag, stacked, left_side=True, lower=T...  40.9 us
  transfers between devices with their start and end apart: 17, of which 17 were waited for; matrix products, arithmetic and copies ran while one was open for 3% of the time, Pallas kernels for 0%

profile of v1, /device:TPU:0, one launch (start us, length us, event | category | flops | bytes accessed | tf_op | source)
XLA Modules:
  0.0 1355.7 jit_solution(3204495361882074598)
XLA Ops:
  7.4 1.9 bitcast_select_fusion.2
  10.4 78.6 %all-gather.48.cloned.1.call-done = f32[16,1,256,256]{3,2,1,0:T(8,128)} async-done(((f32[1,1,256,256]{3,2,1,0:T(8,128)}), f32[16,1,256,256]{3,2,1,0:T(8,128)}) %all-gather.48.cloned.1.call-update) | async-done | bytes 4194320 | tf_op jit(solution)/shard_map/all_gather | solution.py:13
  89.0 2.5 bitcast_reduce_fusion.1
  93.5 11.7 cholesky.130
  106.0 9.8 custom-call.13
  118.0 11.7 cholesky.147
  132.5 4.4 while.6
  137.0 19.7 %custom-call.14 = f32[2,128,128]{1,2,0:T(8,128)S(1)} custom-call(f32[2,128,128]{2,1,0:T(8,128)S(1)} %get-tuple-element.45), custom_call_target="InvertDiagBlocksLowerTriangular" | custom-call | tf_op jit(solution)/shard_map/triangular_solve/custom-call.0 | solution.py:22
  158.1 1.9 select_select_fusion.1
  160.1 7.7 all-gather.50.cloned.1.call-done
  175.4 72.4 %all-gather.24.cloned.1.call-done = f32[16,256,256]{2,1,0:T(8,128)} async-done(((f32[1,256,256]{2,1,0:T(8,128)}), f32[16,256,256]{2,1,0:T(8,128)}) %all-gather.24.cloned.1.call-update) | async-done | bytes 4194320 | tf_op jit(solution)/shard_map/all_gather | solution.py:13
  247.9 2.5 reduce_sum.161
  250.4 74.9 %all-gather.26.cloned.1.call-done = f32[16,256,256]{2,1,0:T(8,128)} async-done(((f32[1,256,256]{2,1,0:T(8,128)}), f32[16,256,256]{2,1,0:T(8,128)}) %all-gather.26.cloned.1.call-update) | async-done | bytes 4194320 | tf_op jit(solution)/shard_map/all_gather | solution.py:13
  325.2 2.5 reduce_sum.162
  327.7 74.9 %all-gather.28.cloned.1.call-done = f32[16,256,256]{2,1,0:T(8,128)} async-done(((f32[1,256,256]{2,1,0:T(8,128)}), f32[16,256,256]{2,1,0:T(8,128)}) %all-gather.28.cloned.1.call-update) | async-done | bytes 4194320 | tf_op jit(solution)/shard_map/all_gather | solution.py:13
  402.5 2.5 reduce_sum.163
  405.0 74.9 %all-gather.30.cloned.1.call-done = f32[16,256,256]{2,1,0:T(8,128)} async-done(((f32[1,256,256]{2,1,0:T(8,128)}), f32[16,256,256]{2,1,0:T(8,128)}) %all-gather.30.cloned.1.call-update) | async-done | bytes 4194320 | tf_op jit(solution)/shard_map/all_gather | solution.py:13
  479.9 2.5 reduce_sum.164
  482.4 75.0 %all-gather.32.cloned.1.call-done = f32[16,256,256]{2,1,0:T(8,128)} async-done(((f32[1,256,256]{2,1,0:T(8,128)}), f32[16,256,256]{2,1,0:T(8,128)}) %all-gather.32.cloned.1.call-update) | async-done | bytes 4194320 | tf_op jit(solution)/shard_map/all_gather | solution.py:13
  557.4 2.5 reduce_sum.165
  559.8 75.0 %all-gather.22.cloned.1.call-done = f32[16,256,256]{2,1,0:T(8,128)} async-done(((f32[1,256,256]{2,1,0:T(8,128)}), f32[16,256,256]{2,1,0:T(8,128)}) %all-gather.22.cloned.1.call-update) | async-done | bytes 4194320 | tf_op jit(solution)/shard_map/all_gather | solution.py:13
  634.9 2.5 reduce_sum.160
  641.6 70.7 %all-gather.34.cloned.1.call-done = f32[16,256,256]{2,1,0:T(8,128)} async-done(((f32[1,256,256]{2,1,0:T(8,128)}), f32[16,256,256]{2,1,0:T(8,128)}) %all-gather.34.cloned.1.call-update) | async-done | bytes 4194320 | tf_op jit(solution)/shard_map/all_gather | solution.py:13
  712.3 2.5 reduce_sum.166
  715.6 4.2 fusion.2
  720.9 74.4 %all-gather.52.cloned.1.call-done = f32[16,1,256,256]{3,2,1,0:T(8,128)} async-done(((f32[1,1,256,256]{3,2,1,0:T(8,128)}), f32[16,1,256,256]{3,2,1,0:T(8,128)}) %all-gather.52.cloned.1.call-update) | async-done | bytes 4194320 | tf_op jit(solution)/shard_map/all_gather | solution.py:13
  795.3 2.5 bitcast_reduce_fusion
  799.8 11.7 cholesky.164
  812.3 9.8 custom-call.15
  824.3 11.7 cholesky.181
  838.8 4.2 while.7
  843.0 19.7 %custom-call.16 = f32[2,128,128]{1,2,0:T(8,128)S(1)} custom-call(f32[2,128,128]{2,1,0:T(8,128)S(1)} %get-tuple-element.46), custom_call_target="InvertDiagBlocksLowerTriangular" | custom-call | tf_op jit(solution)/shard_map/triangular_solve/custom-call.0 | solution.py:22
  864.1 1.9 select_select_fusion
  866.1 7.7 all-gather.54.cloned.1.call-done
  880.6 73.3 %all-gather.38.cloned.1.call-done = f32[16,256,256]{2,1,0:T(8,128)} async-done(((f32[1,256,256]{2,1,0:T(8,128)}), f32[16,256,256]{2,1,0:T(8,128)}) %all-gather.38.cloned.1.call-update) | async-done | bytes 4194320 | tf_op jit(solution)/shard_map/all_gather | solution.py:13
  953.9 2.5 reduce_sum.171
  956.3 75.0 %all-gather.40.cloned.1.call-done = f32[16,256,256]{2,1,0:T(8,128)} async-done(((f32[1,256,256]{2,1,0:T(8,128)}), f32[16,256,256]{2,1,0:T(8,128)}) %all-gather.40.cloned.1.call-update) | async-done | bytes 4194320 | tf_op jit(solution)/shard_map/all_gather | solution.py:13
  1031.4 2.5 reduce_sum.172
  1033.8 74.9 %all-gather.42.cloned.1.call-done = f32[16,256,256]{2,1,0:T(8,128)} async-done(((f32[1,256,256]{2,1,0:T(8,128)}), f32[16,256,256]{2,1,0:T(8,128)}) %all-gather.42.cloned.1.call-update) | async-done | bytes 4194320 | tf_op jit(solution)/shard_map/all_gather | solution.py:13
  1108.7 2.5 reduce_sum.173
  1111.2 74.9 %all-gather.44.cloned.1.call-done = f32[16,256,256]{2,1,0:T(8,128)} async-done(((f32[1,256,256]{2,1,0:T(8,128)}), f32[16,256,256]{2,1,0:T(8,128)}) %all-gather.44.cloned.1.call-update) | async-done | bytes 4194320 | tf_op jit(solution)/shard_map/all_gather | solution.py:13
  1186.0 3.2 reduce_sum.174
  1189.2 74.2 %all-gather.36.cloned.1.call-done = f32[16,256,256]{2,1,0:T(8,128)} async-done(((f32[1,256,256]{2,1,0:T(8,128)}), f32[16,256,256]{2,1,0:T(8,128)}) %all-gather.36.cloned.1.call-update) | async-done | bytes 4194320 | tf_op jit(solution)/shard_map/all_gather | solution.py:13
  1263.4 3.2 reduce_sum.170
  1266.6 1.7 bitcast_dynamic-update-slice_fusion.7
  1271.2 69.6 %all-gather.46.cloned.1.call-done = f32[16,256,256]{2,1,0:T(8,128)} async-done(((f32[1,256,256]{2,1,0:T(8,128)}), f32[16,256,256]{2,1,0:T(8,128)}) %all-gather.46.cloned.1.call-update) | async-done | bytes 4194320 | tf_op jit(solution)/shard_map/all_gather | solution.py:13
  1340.7 2.5 reduce_sum.175
  1343.9 3.5 fusion.1
  (133 shorter events, 50.9 us)
Async XLA Ops:
  6.5 82.5 %all-gather.48.cloned.1.call-start = ((), (), s32[]{:S(2)}) async-start(), calls=%async_computation.13 | async-start | bytes 4456448 | tf_op jit(solution)/shard_map/all_gather | solution.py:13
  10.1 157.7 %all-gather.50.cloned.1.call-start = ((), (), s32[]{:S(2)}) async-start(), calls=%async_computation.14 | async-start | bytes 1572864 | tf_op jit(solution)/shard_map/all_gather | solution.py:13
  93.5 12.5 copy-start.2
  160.0 87.9 %all-gather.24.cloned.1.call-start = ((), (), s32[]{:S(2)}) async-start(), calls=%async_computation.1 | async-start | bytes 4456448 | tf_op jit(solution)/shard_map/all_gather | solution.py:13
  170.5 154.7 %all-gather.26.cloned.1.call-start = ((), (), s32[]{:S(2)}) async-start(), calls=%async_computation.2 | async-start | bytes 4456448 | tf_op jit(solution)/shard_map/all_gather | solution.py:13
  171.0 231.5 %all-gather.28.cloned.1.call-start = ((), (), s32[]{:S(2)}) async-start(), calls=%async_computation.3 | async-start | bytes 4456448 | tf_op jit(solution)/shard_map/all_gather | solution.py:13
  171.6 308.3 %all-gather.30.cloned.1.call-start = ((), (), s32[]{:S(2)}) async-start(), calls=%async_computation.4 | async-start | bytes 4456448 | tf_op jit(solution)/shard_map/all_gather | solution.py:13
  172.2 385.2 %all-gather.32.cloned.1.call-start = ((), (), s32[]{:S(2)}) async-start(), calls=%async_computation.5 | async-start | bytes 4456448 | tf_op jit(solution)/shard_map/all_gather | solution.py:13
  173.0 461.9 %all-gather.22.cloned.1.call-start = ((), (), s32[]{:S(2)}) async-start(), calls=%async_computation | async-start | bytes 4456448 | tf_op jit(solution)/shard_map/all_gather | solution.py:13
  173.7 538.6 %all-gather.34.cloned.1.call-start = ((), (), s32[]{:S(2)}) async-start(), calls=%async_computation.6 | async-start | bytes 4456448 | tf_op jit(solution)/shard_map/all_gather | solution.py:13
  174.4 620.9 %all-gather.52.cloned.1.call-start = ((), (), s32[]{:S(2)}) async-start(), calls=%async_computation.15 | async-start | bytes 4456448 | tf_op jit(solution)/shard_map/all_gather | solution.py:13
  175.4 74.9 %copy-start = (f32[2,4,256,256]{3,2,0,1:T(8,128)}, f32[2,4,256,256]{3,2,0,1:T(8,128)S(1)}, u32[]{:S(2)}) copy-start(f32[2,4,256,256]{3,2,0,1:T(8,128)S(1)} %fusion.12) | copy-start | bytes 6291460
  720.5 153.3 %all-gather.54.cloned.1.call-start = ((), (), s32[]{:S(2)}) async-start(), calls=%async_computation.16 | async-start | bytes 1572864 | tf_op jit(solution)/shard_map/all_gather | solution.py:13
  799.8 12.5 copy-start.3
  866.0 87.9 %all-gather.38.cloned.1.call-start = ((), (), s32[]{:S(2)}) async-start(), calls=%async_computation.8 | async-start | bytes 4456448 | tf_op jit(solution)/shard_map/all_gather | solution.py:13
  876.5 154.9 %all-gather.40.cloned.1.call-start = ((), (), s32[]{:S(2)}) async-start(), calls=%async_computation.9 | async-start | bytes 4456448 | tf_op jit(solution)/shard_map/all_gather | solution.py:13
  877.2 231.5 %all-gather.42.cloned.1.call-start = ((), (), s32[]{:S(2)}) async-start(), calls=%async_computation.10 | async-start | bytes 4456448 | tf_op jit(solution)/shard_map/all_gather | solution.py:13
  877.8 308.2 %all-gather.44.cloned.1.call-start = ((), (), s32[]{:S(2)}) async-start(), calls=%async_computation.11 | async-start | bytes 4456448 | tf_op jit(solution)/shard_map/all_gather | solution.py:13
  878.4 385.0 %all-gather.36.cloned.1.call-start = ((), (), s32[]{:S(2)}) async-start(), calls=%async_computation.7 | async-start | bytes 4456448 | tf_op jit(solution)/shard_map/all_gather | solution.py:13
  879.0 461.7 %all-gather.46.cloned.1.call-start = ((), (), s32[]{:S(2)}) async-start(), calls=%async_computation.12 | async-start | bytes 4456448 | tf_op jit(solution)/shard_map/all_gather | solution.py:13
  1266.6 3.9 copy-start.1
Sparse Core Ops, SparseCore 0:
  10.2 78.7 all-gather.47
  160.1 7.6 all-gather.49
  170.6 77.2 all-gather.23
  250.5 74.6 all-gather.25
  327.8 74.6 all-gather.27
  405.2 74.6 all-gather.29
  482.6 74.6 all-gather.31
  560.1 74.6 all-gather.21
  637.6 74.6 all-gather.33
  720.6 74.6 all-gather.51
  866.1 7.6 all-gather.53
  876.6 77.2 all-gather.37
  956.6 74.6 all-gather.39
  1034.0 74.6 all-gather.41
  1111.3 74.6 all-gather.43
  1188.6 74.6 all-gather.35
  1266.0 74.6 all-gather.45
